TPU v7x, 32 devices: a whole 2x2x4 slice. The times are simulated.
32 devices in a mesh: clips: 2 (over x), tm: 8 (over z, y), cols: 2 (over core).
Axes of the slice: x: 2, y: 2, z: 4, core: 2. Of those that a mesh axis runs over, the one named last changes fastest.
Arguments:
- video: bfloat16 [64, 32, 32, 512], P(('clips', 'tm'), None, 'cols'), parts along dimension 0, may hold values from -6 to 6
- w_time: bfloat16 [3, 512, 512], replicated, may hold values from -0.15625 to 0.15625
- b_time: float32 [512], replicated, may hold values from -3 to 3
- w_down: bfloat16 [3, 512, 512], replicated, may hold values from -0.15625 to 0.15625
- b_down: float32 [512], replicated, may hold values from -3 to 3
- w_space: bfloat16 [9, 512, 512], replicated, may hold values from -0.09375 to 0.09375
- b_space: float32 [512], replicated, may hold values from -3 to 3
- gain: float32 [512], replicated, may hold values from 0.1 to 1.9
- w_query: bfloat16 [512, 512], replicated, may hold values from -30 to 30
- w_key: bfloat16 [512, 512], replicated, may hold values from -0.25 to 0.25
- w_value: bfloat16 [512, 512], replicated, may hold values from -0.25 to 0.25
- w_out: bfloat16 [512, 512], replicated, may hold values from -0.25 to 0.25
Outputs:
- encoded: bfloat16 [32, 32, 32, 512], P(('clips', 'tm'), None, 'cols'), parts along dimension 0
There are 2 independent parts, one for each index of `clips`. A program takes and returns all parts, laid end to end along the dimension named above; an argument that names none is the same for every part. Nothing has to cross between parts.
All inputs are finite; a program needn't handle non-finite values.
Results may differ from a plain program's by a relative error of at most 0.019.
The roundings to bfloat16 on the way count: a program that leaves them out, or rounds other values in their place, can miss the bound.
Values may be sent and summed in bfloat16 or wider, within the bound.
A program may use at most 64 MiB of HBM per device.

v0:
```python
from functools import partial

import jax
import jax.numpy as jnp
from jax import lax
from jax.experimental import pallas as pl
from jax.experimental.pallas import tpu as pltpu
from jax.sharding import PartitionSpec as P

epsilon = 1e-06
MESH = pl.DeviceIdType.MESH


def block_kernel(
    shape, video_hbm, wt_hbm, bt, wd_hbm, bd, ws_hbm, bs, gain, wq_hbm, wk_hbm, wv_hbm, wo_hbm, y_ref,
    wt, wd, ws, wq, wk, wv, wo, video, lifted, left_of, middle, right_of,
    edges, halo, spatial, held, done,
    load_sem, frame_send, frame_recv, edge_send, edge_recv, send_sem, recv_sem, back_sem, home_sem,
):
    height, strip = shape
    frames, area, channels = video_hbm.shape
    halves, chunks, owners, pixels, _ = y_ref.shape
    total = owners * halves
    rows = total * pixels
    me, col, cols = lax.axis_index("tm"), lax.axis_index("cols"), lax.axis_size("cols")
    f32, bf16 = jnp.float32, jnp.bfloat16
    tile = owners * pixels
    lines = tile // strip

    loads = [
        pltpu.make_async_copy(source, target, load_sem.at[i])
        for i, (source, target) in enumerate(
            (
                (video_hbm, video.at[pl.ds(2, frames)]), (wt_hbm, wt), (wd_hbm, wd), (ws_hbm, ws),
                (wq_hbm, wq), (wk_hbm, wk), (wv_hbm, wv), (wo_hbm, wo),
            )
        )
    ]
    for load in loads:
        load.start()

    barrier = pltpu.get_barrier_semaphore()

    def greet(k, _):
        peer = lax.rem(me + k, owners)
        pl.semaphore_signal(barrier, inc=1, device_id={"tm": peer}, device_id_type=MESH)
        return 0

    lax.fori_loop(1, owners, greet, 0)

    def greet_side(k, _):
        peer = lax.rem(col + k, cols)
        pl.semaphore_signal(barrier, inc=1, device_id={"cols": peer}, device_id_type=MESH)
        return 0

    lax.fori_loop(1, cols, greet_side, 0)
    pl.semaphore_wait(barrier, owners + cols - 2)

    has_next, has_before = me < owners - 1, me > 0

    def span(b):
        return pl.ds(b * tile, tile)

    def landing(i, b):
        return (video.at[1, span(b)], video.at[0, span(b)], lifted.at[0, span(b)])[i]

    def onward(i, b):
        source = (video.at[frames + 1, span(b)], video.at[frames, span(b)], lifted.at[frames, span(b)])[i]
        return pltpu.make_async_remote_copy(
            src_ref=source, dst_ref=landing(i, b),
            send_sem=frame_send.at[i, b], recv_sem=frame_recv.at[i, b],
            device_id={"tm": lax.rem(me + 1, owners)}, device_id_type=MESH,
        )

    def send_on(i, b):
        @pl.when(has_next)
        def _():
            onward(i, b).start()

    def take(i, b):
        @pl.when(has_before)
        def _():
            onward(i, b).wait_recv()

        @pl.when(jnp.logical_not(has_before))
        def _():
            landing(i, b)[...] = jnp.zeros((tile, channels), bf16)

    def stacked(ref, which, b):
        return jnp.concatenate([ref[f, span(b)] for f in which], 0)

    def lift(first, count, b):
        own = [f + 2 for f in range(first, first + count)]
        summed = jnp.dot(stacked(video, own, b), wt[0], preferred_element_type=f32)
        for k in (1, 2):
            summed = summed + jnp.dot(
                stacked(video, [f - k for f in own], b), wt[k], preferred_element_type=f32
            )
        summed = summed + bt[...]
        result = (stacked(video, own, b).astype(f32) + jax.nn.silu(summed)).astype(bf16)
        for i in range(count):
            lifted[first + 1 + i, span(b)] = result[i * tile : (i + 1) * tile]

    def sideways(b, side):
        peer = lax.rem(col + 1, cols) if side == 0 else lax.rem(col + cols - 1, cols)
        return pltpu.make_async_remote_copy(
            src_ref=edges.at[b, side], dst_ref=halo.at[b, side],
            send_sem=edge_send.at[b, side], recv_sem=edge_recv.at[b, side],
            device_id={"cols": peer}, device_id_type=MESH,
        )

    sends_side = (col < cols - 1, col > 0)
    takes_side = (col > 0, col < cols - 1)

    def window(ref, b, a):
        start = b * lines + a
        return ref[:, start : start + lines].reshape(halves * tile, channels)

    def place_band(ref, b, value):
        ref[:, 1 + b * lines : 1 + (b + 1) * lines] = value.reshape(halves, lines, strip, channels)

    def reduce_band(b):
        summed = jnp.zeros((halves * tile, channels), f32) + bd[...]
        for k in range(3):
            which = [2 * s + 2 - k for s in range(halves)]
            summed = summed + jnp.dot(stacked(lifted, which, b), wd[k], preferred_element_type=f32)
        reduced = summed.astype(bf16)
        place_band(middle, b, reduced)
        wide = reduced.astype(f32).reshape(halves, lines, strip, channels)
        edges[b, 0] = wide[:, :, strip - 1].astype(bf16)
        edges[b, 1] = wide[:, :, 0].astype(bf16)
        for side in range(2):
            @pl.when(sends_side[side])
            def _():
                sideways(b, side).start()

    def shift_band(b):
        for side in range(2):
            @pl.when(takes_side[side])
            def _():
                sideways(b, side).wait_recv()

            @pl.when(jnp.logical_not(takes_side[side]))
            def _():
                halo[b, side] = jnp.zeros((halves, lines, channels), bf16)

        size = halves * tile
        wide = window(middle, b, 1).astype(f32)
        place = lax.rem(lax.broadcasted_iota(jnp.int32, (size, channels), 0), strip)

        def spread(side):
            column = halo[b, side].astype(f32)
            column = jnp.broadcast_to(column[:, :, None, :], (halves, lines, strip, channels))
            return column.reshape(size, channels)

        lower = jnp.where(place == 0, spread(0), pltpu.roll(wide, 1, 0))
        upper = jnp.where(place == strip - 1, spread(1), pltpu.roll(wide, size - 1, 0))
        place_band(left_of, b, lower.astype(bf16))
        place_band(right_of, b, upper.astype(bf16))

    def convolve_band(b):
        summed = jnp.zeros((halves * tile, channels), f32) + bs[...]
        for k, shifted in ((1, middle), (0, left_of), (2, right_of)):
            for a in range(3):
                summed = summed + jnp.dot(
                    window(shifted, b, a), ws[3 * a + k], preferred_element_type=f32
                )
        result = (window(middle, b, 1).astype(f32) + jax.nn.silu(summed)).astype(bf16)
        spatial[b] = result.reshape(halves, owners, pixels, channels)

    def outward(c, peer, slot, source):
        return pltpu.make_async_remote_copy(
            src_ref=spatial.at[c, :, peer],
            dst_ref=held.at[c, source],
            send_sem=send_sem.at[c, slot],
            recv_sem=recv_sem.at[c, source],
            device_id={"tm": peer},
            device_id_type=MESH,
        )

    def homeward(c, peer, slot, source):
        return pltpu.make_async_remote_copy(
            src_ref=done.at[c, peer],
            dst_ref=y_ref.at[:, c, source],
            send_sem=back_sem.at[c, slot],
            recv_sem=home_sem.at[c, source],
            device_id={"tm": peer},
            device_id_type=MESH,
        )

    def scatter(c):
        def send(k, _):
            outward(c, lax.rem(me + k, owners), k, me).start()
            return 0

        lax.fori_loop(1, owners, send, 0)

    def attend(c):
        held[c, me] = spatial[c, :, me]

        def arrive(k, _):
            source = lax.rem(me + owners - k, owners)
            outward(c, lax.rem(me + k, owners), k, source).wait_recv()
            return 0

        lax.fori_loop(1, owners, arrive, 0)
        place = lax.broadcasted_iota(jnp.int32, (rows, rows), 0)
        other = lax.broadcasted_iota(jnp.int32, (rows, rows), 1)
        allowed = (lax.rem(place, pixels) == lax.rem(other, pixels)) & (other <= place)
        wide = held[c].reshape(rows, channels).astype(f32)
        scale = lax.rsqrt(jnp.mean(wide * wide, axis=-1, keepdims=True) + epsilon)
        normed = (wide * scale * gain[...]).astype(bf16)
        query = jnp.dot(normed, wq[...], preferred_element_type=f32).astype(bf16)
        key = jnp.dot(normed, wk[...], preferred_element_type=f32).astype(bf16)
        value = jnp.dot(normed, wv[...], preferred_element_type=f32).astype(bf16)
        scores = lax.dot_general(
            query, key, (((1,), (1,)), ((), ())), preferred_element_type=f32
        ) * channels ** (-0.5)
        scores = jnp.where(allowed, scores, -1e30)
        largest = jnp.max(scores, axis=-1, keepdims=True)
        probs = jnp.exp(scores - largest)
        probs = (probs / jnp.sum(probs, axis=-1, keepdims=True)).astype(bf16)
        context = jnp.dot(probs, value, preferred_element_type=f32).astype(bf16)
        mixed = jnp.dot(context, wo[...], preferred_element_type=f32)
        result = (wide + mixed).astype(bf16)
        done[c] = result.reshape(owners, halves, pixels, channels)

        def back(k, _):
            homeward(c, lax.rem(me + k, owners), k, me).start()
            return 0

        lax.fori_loop(1, owners, back, 0)
        y_ref[:, c, me] = done[c, me]

    for shifted in (left_of, middle, right_of):
        for line in (0, height + 1):
            shifted[:, line] = jnp.zeros((halves, strip, channels), bf16)
    loads[0].wait()
    send_on(0, 0)
    send_on(1, 0)
    loads[1].wait()
    for b in range(chunks):
        lift(2, frames - 2, b)
        send_on(2, b)
        if b + 1 < chunks:
            send_on(0, b + 1)
            send_on(1, b + 1)
    for load in loads[2:]:
        load.wait()
    for b in range(chunks + 1):
        if b < chunks:
            take(0, b)
            take(1, b)
            lift(0, 2, b)
            take(2, b)
            reduce_band(b)
            shift_band(b)
        if b >= 1:
            if b == chunks and chunks > 1:
                attend(0)
            convolve_band(b - 1)
            scatter(b - 1)
    for c in range(min(1, chunks - 1), chunks):
        attend(c)

    @pl.when(has_next)
    def _():
        for b in range(chunks):
            for i in range(3):
                onward(i, b).wait_send()

    for b in range(chunks):
        for side in range(2):
            @pl.when(sends_side[side])
            def _():
                sideways(b, side).wait_send()

    for c in range(chunks):
        def finish(k, _):
            peer, source = lax.rem(me + k, owners), lax.rem(me + owners - k, owners)
            outward(c, peer, k, me).wait_send()
            homeward(c, peer, k, me).wait_send()
            homeward(c, peer, k, source).wait_recv()
            return 0

        lax.fori_loop(1, owners, finish, 0)


def per_device(
    video, w_time, b_time, w_down, b_down, w_space, b_space, gain, w_query, w_key, w_value, w_out
):
    frames, height, strip, channels = video.shape
    halves, owners, area = frames // 2, lax.axis_size("tm"), height * strip
    owned = area // owners
    pixels = min(16, owned)
    chunks = owned // pixels
    vmem = pl.BlockSpec(memory_space=pltpu.VMEM)
    hbm = pl.BlockSpec(memory_space=pltpu.HBM)
    bf16 = jnp.bfloat16
    square = (channels, channels)
    shifted = pltpu.VMEM((halves, height + 2, strip, channels), bf16)
    flat = lambda v: v.reshape(1, channels)
    sems = pltpu.SemaphoreType.DMA
    result = pl.pallas_call(
        partial(block_kernel, (height, strip)),
        out_shape=jax.ShapeDtypeStruct((halves, chunks, owners, pixels, channels), bf16),
        in_specs=[hbm, hbm, vmem, hbm, vmem, hbm, vmem, vmem, hbm, hbm, hbm, hbm],
        out_specs=vmem,
        scratch_shapes=[
            pltpu.VMEM((3,) + square, bf16),
            pltpu.VMEM((3,) + square, bf16),
            pltpu.VMEM((9,) + square, bf16),
            pltpu.VMEM(square, bf16),
            pltpu.VMEM(square, bf16),
            pltpu.VMEM(square, bf16),
            pltpu.VMEM(square, bf16),
            pltpu.VMEM((frames + 2, area, channels), bf16),
            pltpu.VMEM((frames + 1, area, channels), bf16),
            shifted,
            shifted,
            shifted,
            pltpu.VMEM((chunks, 2, halves, height // chunks, channels), bf16),
            pltpu.VMEM((chunks, 2, halves, height // chunks, channels), bf16),
            pltpu.VMEM((chunks, halves, owners, pixels, channels), bf16),
            pltpu.VMEM((chunks, owners, halves, pixels, channels), bf16),
            pltpu.VMEM((chunks, owners, halves, pixels, channels), bf16),
            sems((8,)),
            sems((3, chunks)),
            sems((3, chunks)),
            sems((chunks, 2)),
            sems((chunks, 2)),
            sems((chunks, owners)),
            sems((chunks, owners)),
            sems((chunks, owners)),
            sems((chunks, owners)),
        ],
        compiler_params=pltpu.CompilerParams(
            collective_id=0, has_side_effects=True, vmem_limit_bytes=57 * 1024 * 1024
        ),
    )(
        video.reshape(frames, area, channels), w_time, flat(b_time), w_down, flat(b_down),
        w_space, flat(b_space), flat(gain), w_query, w_key, w_value, w_out,
    )
    return result.reshape(halves, height, strip, channels)


def solution(mesh):
    return jax.shard_map(
        per_device,
        mesh=mesh,
        in_specs=(P(("clips", "tm"), None, "cols", None),) + (P(),) * 11,
        out_specs=P(("clips", "tm"), None, "cols", None),
        check_vma=False,
    )
```

profile of v0, /device:TPU:27, one launch (start us, length us, event | category | flops | bytes accessed | tf_op | source)
XLA Modules:
  0.0 89.2 jit_solution(11506931904988292138)
XLA Ops:
  0.0 86.9 %shard_map.118 = bf16[2,4,8,16,512]{4,3,2,1,0:T(8,128)(2,1)} custom-call(bf16[4,512,512]{2,1,0:T(8,128)(2,1)} %bitcast.7, bf16[3,512,512]{2,1,0:T(8,128)(2,1)} %wt_hbm.1, f32[1,512]{1,0:T(1,128)} %bitcast.8, bf16[3,512,512]{2,1,0:T(8,128)(2,1)} %wd_hbm.1, f32[1,512]{1,0:T(1,128)} %bitcast.9, bf16[9,512,512]{2,1,0:T(8,128)(2,1)} %ws_hbm.1, ...), custom_call_target="tpu_custom_call" | custom-call | tf_op jit(solution)/shard_map/pallas_call | solution.py:304
  86.9 2.3 %copy.14 = bf16[2,32,16,512]{3,2,1,0:T(8,128)(2,1)} copy(bf16[2,32,16,512]{3,2,1,0:T(8,128)(2,1)} %bitcast.6) | data formatting | bytes 2097152
where the time goes:
time: 89.4 us; the launch traced here: 89.2 us
  Pallas kernels  86.9 us (97%)
  local copies, waits for them, and re-layouts  2.26 us (3%)
    pallas_call x1, Pallas kernels, per_device(): pl.pallas_call(partial(block_kernel, (height, strip)), out_shape=jax.Shap...  86.9 us
    unnamed x1, local copies, waits for them, and re-layouts  2.26 us

commit v1 on v0

v1 whole, which is shorter than its diff:
```python
from functools import partial

import jax
import jax.numpy as jnp
from jax import lax
from jax.experimental import pallas as pl
from jax.experimental.pallas import tpu as pltpu
from jax.sharding import PartitionSpec as P

epsilon = 1e-06
MESH = pl.DeviceIdType.MESH


def block_kernel(
    shape, video_hbm, wt_hbm, bt, wd_hbm, bd, ws_hbm, bs, gain, wq_hbm, wk_hbm, wv_hbm, wo_hbm, y_ref,
    wt, wd, ws, wq, wk, wv, wo, video, lifted, left_of, middle, right_of,
    edges, halo, relayed, spatial, held, done,
    load_sem, up_send, up_recv, down_send, down_recv, pass_send, pass_recv, edge_send, edge_recv,
    send_sem, recv_sem, back_sem, home_sem,
):
    height, strip = shape
    frames, area, channels = video_hbm.shape
    halves, chunks, owners, pixels, _ = y_ref.shape
    total = owners * halves
    rows = total * pixels
    me, col, cols = lax.axis_index("tm"), lax.axis_index("cols"), lax.axis_size("cols")
    f32, bf16 = jnp.float32, jnp.bfloat16
    bands, padded = edges.shape[1], edges.shape[3]
    share = chunks // bands
    lines = height // bands
    starts = [0] + [b * lines + 1 for b in range(1, bands)] + [height]
    relays = owners % 2 == 0 and owners > 2

    loads = [
        pltpu.make_async_copy(source, target, load_sem.at[i])
        for i, (source, target) in enumerate(
            (
                (video_hbm, video.at[pl.ds(1, frames)]), (wt_hbm, wt), (wd_hbm, wd), (ws_hbm, ws),
                (wq_hbm, wq), (wk_hbm, wk), (wv_hbm, wv), (wo_hbm, wo),
            )
        )
    ]
    for load in loads:
        load.start()

    barrier = pltpu.get_barrier_semaphore()

    def greet(k, _):
        peer = lax.rem(me + k, owners)
        pl.semaphore_signal(barrier, inc=1, device_id={"tm": peer}, device_id_type=MESH)
        return 0

    lax.fori_loop(1, owners, greet, 0)

    def greet_side(k, _):
        peer = lax.rem(col + k, cols)
        pl.semaphore_signal(barrier, inc=1, device_id={"cols": peer}, device_id_type=MESH)
        return 0

    lax.fori_loop(1, cols, greet_side, 0)

    for j in range(halves + 1):
        for shifted in (left_of, middle, right_of):
            for line in (0, height + 1):
                shifted[j, line] = jnp.zeros((strip, channels), bf16)

    has_next, has_before = me < owners - 1, me > 0
    even = lax.rem(me, 2) == 0

    @pl.when(jnp.logical_not(has_before))
    def _():
        video[0] = jnp.zeros((area, channels), bf16)

    @pl.when(jnp.logical_not(has_next))
    def _():
        for i in range(2):
            video[frames + 1 + i] = jnp.zeros((area, channels), bf16)

    pl.semaphore_wait(barrier, owners + cols - 2)

    def span(b):
        return pl.ds(starts[b] * strip, (starts[b + 1] - starts[b]) * strip)

    def remote(source, target, sent, landed, peer):
        return pltpu.make_async_remote_copy(
            src_ref=source, dst_ref=target, send_sem=sent, recv_sem=landed,
            device_id={"tm": peer}, device_id_type=MESH,
        )

    def upward(b):
        peer = lax.rem(me + 1, owners)
        return remote(video.at[frames, span(b)], video.at[0, span(b)], up_send.at[b], up_recv.at[b], peer)

    def downward(i, b):
        peer = lax.rem(me + owners - 1, owners)
        return remote(
            video.at[1 + i, span(b)], video.at[frames + 1 + i, span(b)],
            down_send.at[i, b], down_recv.at[i, b], peer,
        )

    def aside(b):
        peer = lax.rem(me + 1, owners)
        return remote(video.at[2, span(b)], relayed.at[span(b)], down_send.at[1, b], pass_recv.at[b], peer)

    def onward(b):
        peer = lax.rem(me + owners - 2, owners)
        return remote(
            relayed.at[span(b)], video.at[frames + 2, span(b)], pass_send.at[b], down_recv.at[1, b], peer
        )

    turns = even & has_before if relays else me < 0
    passes = jnp.logical_not(even) & (me > 2) if relays else me < 0
    straight = has_before & jnp.logical_not(turns)

    def send_halos():
        for b in range(bands):
            @pl.when(has_next)
            def _():
                upward(b).start()
        for b in range(bands):
            @pl.when(has_before)
            def _():
                downward(0, b).start()

            @pl.when(straight)
            def _():
                downward(1, b).start()

            @pl.when(turns)
            def _():
                aside(b).start()

    def pass_on(b):
        @pl.when(passes)
        def _():
            aside(b).wait_recv()
            onward(b).start()

    def stacked(ref, which, b):
        return jnp.concatenate([ref[f, span(b)] for f in which], 0)

    def lift(first, count, b):
        size = (starts[b + 1] - starts[b]) * strip
        own = [f + 1 for f in range(first, first + count)]
        summed = jnp.dot(stacked(video, own, b), wt[0], preferred_element_type=f32)
        for k in (1, 2) if first else ():
            summed = summed + jnp.dot(
                stacked(video, [f - k for f in own], b), wt[k], preferred_element_type=f32
            )
        summed = summed + bt[...]
        result = (stacked(video, own, b).astype(f32) + jax.nn.silu(summed)).astype(bf16)
        for i in range(count):
            lifted[first + i, span(b)] = result[i * size : (i + 1) * size]

    def sideways(j, b, side):
        peer = lax.rem(col + 1, cols) if side == 0 else lax.rem(col + cols - 1, cols)
        return pltpu.make_async_remote_copy(
            src_ref=edges.at[j, b, side], dst_ref=halo.at[j, b, side],
            send_sem=edge_send.at[j, b, side], recv_sem=edge_recv.at[j, b, side],
            device_id={"cols": peer}, device_id_type=MESH,
        )

    sends_side = (col < cols - 1, col > 0)
    takes_side = (col > 0, col < cols - 1)

    def window(ref, j, start, count):
        return ref[j, start : start + count].reshape(count * strip, channels)

    def reduce_band(j, b):
        first, last = starts[b], starts[b + 1]
        count = last - first
        summed = jnp.zeros((count * strip, channels), f32) + bd[...]
        for k in range(3 if j else 2):
            summed = summed + jnp.dot(
                lifted[2 * j + 1 - k, span(b)], wd[k], preferred_element_type=f32
            )
        reduced = summed.astype(bf16)
        middle[j, 1 + first : 1 + last] = reduced.reshape(count, strip, channels)
        wide = reduced.astype(f32).reshape(count, strip, channels)
        rest = jnp.zeros((padded - count, channels), f32)
        for side, place in ((0, strip - 1), (1, 0)):
            column = wide[:, place]
            column = jnp.concatenate([column, rest], 0) if padded > count else column
            edges[j, b, side] = column.astype(bf16)
        for side in range(2):
            @pl.when(sends_side[side])
            def _():
                sideways(j, b, side).start()

    def shift_band(j, b):
        for side in range(2):
            @pl.when(takes_side[side])
            def _():
                sideways(j, b, side).wait_recv()

            @pl.when(jnp.logical_not(takes_side[side]))
            def _():
                halo[j, b, side] = jnp.zeros((padded, channels), bf16)

        first, last = starts[b], starts[b + 1]
        count = last - first
        size = count * strip
        wide = window(middle, j, 1 + first, count).astype(f32)
        place = lax.rem(lax.broadcasted_iota(jnp.int32, (size, channels), 0), strip)

        def spread(side):
            column = halo[j, b, side].astype(f32)[:count]
            column = jnp.broadcast_to(column[:, None, :], (count, strip, channels))
            return column.reshape(size, channels)

        lower = jnp.where(place == 0, spread(0), pltpu.roll(wide, 1, 0))
        upper = jnp.where(place == strip - 1, spread(1), pltpu.roll(wide, size - 1, 0))
        left_of[j, 1 + first : 1 + last] = lower.astype(bf16).reshape(count, strip, channels)
        right_of[j, 1 + first : 1 + last] = upper.astype(bf16).reshape(count, strip, channels)

    def convolve_band(j, b):
        first = b * lines
        summed = jnp.zeros((lines * strip, channels), f32) + bs[...]
        for k, shifted in ((1, middle), (0, left_of), (2, right_of)):
            for a in range(3):
                summed = summed + jnp.dot(
                    window(shifted, j, first + a, lines), ws[3 * a + k], preferred_element_type=f32
                )
        result = (window(middle, j, 1 + first, lines).astype(f32) + jax.nn.silu(summed)).astype(bf16)
        spatial[j, b * share : (b + 1) * share] = result.reshape(share, owners, pixels, channels)

    def outward(j, c, peer, slot, frame):
        return remote(
            spatial.at[j, c, peer], held.at[c, frame], send_sem.at[j, c, slot], recv_sem.at[c, frame], peer
        )

    def homeward(c, peer, slot, source):
        return remote(
            done.at[c, peer], y_ref.at[:, c, source], back_sem.at[c, slot], home_sem.at[c, source], peer
        )

    def in_use(j):
        return me == 0 if j == 0 else has_next if j == halves else me >= 0

    def scatter(j, c):
        def send(k, _):
            outward(j, c, lax.rem(me + k, owners), k, halves * me + j).start()
            return 0

        @pl.when(in_use(j))
        def _():
            lax.fori_loop(1, owners, send, 0)

    def attend(c):
        for j in range(halves + 1):
            @pl.when(in_use(j))
            def _():
                held[c, halves * me + j] = spatial[j, c, me]

        def arrive(f, _):
            source = lax.div(jnp.maximum(f - 1, 0), halves)

            @pl.when(source != me)
            def _():
                outward(0, c, lax.rem(me + 1, owners), 0, f).wait_recv()

            return 0

        lax.fori_loop(0, total, arrive, 0)
        place = lax.broadcasted_iota(jnp.int32, (rows, rows), 0)
        other = lax.broadcasted_iota(jnp.int32, (rows, rows), 1)
        allowed = (lax.rem(place, pixels) == lax.rem(other, pixels)) & (other <= place)
        wide = held[c].reshape(rows, channels).astype(f32)
        scale = lax.rsqrt(jnp.mean(wide * wide, axis=-1, keepdims=True) + epsilon)
        normed = (wide * scale * gain[...]).astype(bf16)
        query = jnp.dot(normed, wq[...], preferred_element_type=f32).astype(bf16)
        key = jnp.dot(normed, wk[...], preferred_element_type=f32).astype(bf16)
        value = jnp.dot(normed, wv[...], preferred_element_type=f32).astype(bf16)
        scores = lax.dot_general(
            query, key, (((1,), (1,)), ((), ())), preferred_element_type=f32
        ) * channels ** (-0.5)
        scores = jnp.where(allowed, scores, -1e30)
        largest = jnp.max(scores, axis=-1, keepdims=True)
        probs = jnp.exp(scores - largest)
        probs = (probs / jnp.sum(probs, axis=-1, keepdims=True)).astype(bf16)
        context = jnp.dot(probs, value, preferred_element_type=f32).astype(bf16)
        mixed = jnp.dot(context, wo[...], preferred_element_type=f32)
        result = (wide + mixed).astype(bf16)
        done[c] = result.reshape(owners, halves, pixels, channels)

        def back(k, _):
            homeward(c, lax.rem(me + k, owners), k, me).start()
            return 0

        lax.fori_loop(1, owners, back, 0)
        y_ref[:, c, me] = done[c, me]

    loads[0].wait()
    send_halos()
    for load in loads[1:]:
        load.wait()

    def finish_band(j, b):
        shift_band(j, b)
        convolve_band(j, b)
        for c in range(b * share, (b + 1) * share):
            scatter(j, c)

    @pl.when(jnp.logical_not(has_before))
    def _():
        for b in range(bands):
            lift(0, 1, b)
            lift(1, 1, b)
            reduce_band(0, b)
        for b in range(bands):
            finish_band(0, b)

    lift(2, frames - 2, 0)
    for j in range(1, halves + 1):
        for b in range(bands):
            if j == halves:
                pass_on(b)
            if j == 1:
                @pl.when(has_before)
                def _():
                    upward(b).wait_recv()
                    lift(1, 1, b)
            if j == halves:
                @pl.when(has_next)
                def _():
                    for i in range(2):
                        downward(i, b).wait_recv()

                lift(frames, 2, b)
            reduce_band(j, b)
            if j == 1 and b + 1 < bands:
                lift(2, frames - 2, b + 1)
            finish_band(j, b)
    for c in range(chunks):
        attend(c)

    for b in range(bands):
        @pl.when(has_next)
        def _():
            upward(b).wait_send()

        @pl.when(has_before)
        def _():
            for i in range(2):
                downward(i, b).wait_send()

        @pl.when(passes)
        def _():
            onward(b).wait_send()

    for j in range(halves + 1):
        for b in range(bands):
            for side in range(2):
                @pl.when(sends_side[side] & (me == 0) if j == 0 else sends_side[side])
                def _():
                    sideways(j, b, side).wait_send()

    for c in range(chunks):
        for j in range(halves + 1):
            def left(k, _):
                outward(j, c, lax.rem(me + k, owners), k, 0).wait_send()
                return 0

            @pl.when(in_use(j))
            def _():
                lax.fori_loop(1, owners, left, 0)

        def finish(k, _):
            peer, source = lax.rem(me + k, owners), lax.rem(me + owners - k, owners)
            homeward(c, peer, k, me).wait_send()
            homeward(c, peer, k, source).wait_recv()
            return 0

        lax.fori_loop(1, owners, finish, 0)


def per_device(
    video, w_time, b_time, w_down, b_down, w_space, b_space, gain, w_query, w_key, w_value, w_out
):
    frames, height, strip, channels = video.shape
    halves, owners, area = frames // 2, lax.axis_size("tm"), height * strip
    owned = area // owners
    pixels = min(16, owned)
    chunks = owned // pixels
    bands = 2 if chunks % 2 == 0 else 1
    padded = -(-(height // bands + bands - 1) // 8) * 8
    vmem = pl.BlockSpec(memory_space=pltpu.VMEM)
    hbm = pl.BlockSpec(memory_space=pltpu.HBM)
    bf16 = jnp.bfloat16
    square = (channels, channels)
    slots = halves + 1
    shifted = pltpu.VMEM((slots, height + 2, strip, channels), bf16)
    flat = lambda v: v.reshape(1, channels)
    sems = pltpu.SemaphoreType.DMA
    result = pl.pallas_call(
        partial(block_kernel, (height, strip)),
        out_shape=jax.ShapeDtypeStruct((halves, chunks, owners, pixels, channels), bf16),
        in_specs=[hbm, hbm, vmem, hbm, vmem, hbm, vmem, vmem, hbm, hbm, hbm, hbm],
        out_specs=vmem,
        scratch_shapes=[
            pltpu.VMEM((3,) + square, bf16),
            pltpu.VMEM((3,) + square, bf16),
            pltpu.VMEM((9,) + square, bf16),
            pltpu.VMEM(square, bf16),
            pltpu.VMEM(square, bf16),
            pltpu.VMEM(square, bf16),
            pltpu.VMEM(square, bf16),
            pltpu.VMEM((frames + 3, area, channels), bf16),
            pltpu.VMEM((frames + 2, area, channels), bf16),
            shifted,
            shifted,
            shifted,
            pltpu.VMEM((slots, bands, 2, padded, channels), bf16),
            pltpu.VMEM((slots, bands, 2, padded, channels), bf16),
            pltpu.VMEM((area, channels), bf16),
            pltpu.VMEM((slots, chunks, owners, pixels, channels), bf16),
            pltpu.VMEM((chunks, owners * halves, pixels, channels), bf16),
            pltpu.VMEM((chunks, owners, halves, pixels, channels), bf16),
            sems((8,)),
            sems((bands,)),
            sems((bands,)),
            sems((2, bands)),
            sems((2, bands)),
            sems((bands,)),
            sems((bands,)),
            sems((slots, bands, 2)),
            sems((slots, bands, 2)),
            sems((slots, chunks, owners)),
            sems((chunks, owners * halves)),
            sems((chunks, owners)),
            sems((chunks, owners)),
        ],
        compiler_params=pltpu.CompilerParams(
            collective_id=0, has_side_effects=True, vmem_limit_bytes=57 * 1024 * 1024
        ),
    )(
        video.reshape(frames, area, channels), w_time, flat(b_time), w_down, flat(b_down),
        w_space, flat(b_space), flat(gain), w_query, w_key, w_value, w_out,
    )
    return result.reshape(halves, height, strip, channels)


def solution(mesh):
    return jax.shard_map(
        per_device,
        mesh=mesh,
        in_specs=(P(("clips", "tm"), None, "cols", None),) + (P(),) * 11,
        out_specs=P(("clips", "tm"), None, "cols", None),
        check_vma=False,
    )
```

time: 89.4 us -> 99.2 us (1.11); the launches traced: 89.2 us -> 97.4 us
  Pallas kernels: 86.9 us -> 95.2 us
    pallas_call x1, Pallas kernels: 86.9 us -> 95.2 us  [per_device(): pl.pallas_call(partial(block_kernel, (height, strip)), out_shape=jax.Shap...]
where the time goes in v1:
time: 99.2 us; the launch traced here: 97.4 us
  Pallas kernels  95.2 us (96%)
  local copies, waits for them, and re-layouts  2.26 us (2%)
    pallas_call x1, Pallas kernels, per_device(): pl.pallas_call(partial(block_kernel, (height, strip)), out_shape=jax.Shap...  95.2 us
    unnamed x1, local copies, waits for them, and re-layouts  2.26 us

profile of v1, /device:TPU:27, one launch (start us, length us, event | category | flops | bytes accessed | tf_op | source)
XLA Modules:
  0.0 97.4 jit_solution(8200459743333226472)
XLA Ops:
  0.0 95.2 %shard_map.118 = bf16[2,4,8,16,512]{4,3,2,1,0:T(8,128)(2,1)} custom-call(bf16[4,512,512]{2,1,0:T(8,128)(2,1)} %bitcast.7, bf16[3,512,512]{2,1,0:T(8,128)(2,1)} %wt_hbm.1, f32[1,512]{1,0:T(1,128)} %bitcast.8, bf16[3,512,512]{2,1,0:T(8,128)(2,1)} %wd_hbm.1, f32[1,512]{1,0:T(1,128)} %bitcast.9, bf16[9,512,512]{2,1,0:T(8,128)(2,1)} %ws_hbm.1, ...), custom_call_target="tpu_custom_call" | custom-call | tf_op jit(solution)/shard_map/pallas_call | solution.py:395
  95.2 2.3 %copy.14 = bf16[2,32,16,512]{3,2,1,0:T(8,128)(2,1)} copy(bf16[2,32,16,512]{3,2,1,0:T(8,128)(2,1)} %bitcast.6) | data formatting | bytes 2097152

commit v2 on v0

v2 whole, which is shorter than its diff:
```python
import jax
import jax.numpy as jnp
from jax import lax
from jax.experimental import pallas as pl
from jax.experimental.pallas import tpu as pltpu
from jax.sharding import PartitionSpec as P

epsilon = 1e-06
MESH = pl.DeviceIdType.MESH


def block_kernel(
    video_hbm, wt_hbm, bt, wd_hbm, bd, ws_hbm, bs, gain, wq_hbm, wk_hbm, wv_hbm, wo_hbm, y_ref,
    wt, wd, ws, wq, wk, wv, wo, video, lifted, left_of, middle, right_of,
    edges, halo, spatial, held, done,
    load_sem, trade_send, trade_recv, up_send, up_recv, down_send, down_recv, edge_send, edge_recv,
    send_sem, recv_sem, back_sem, home_sem,
):
    frames, height, strip, channels = video_hbm.shape
    halves, _, chunks, groups, pixels, _ = y_ref.shape
    owners, ours = 2 * groups, 2 * halves
    total = groups * ours
    rows = total * pixels
    half = height // 2
    lines = half // chunks
    padded = edges.shape[3]
    me, col, cols = lax.axis_index("tm"), lax.axis_index("cols"), lax.axis_size("cols")
    group, part = lax.div(me, 2), lax.rem(me, 2)
    f32, bf16 = jnp.float32, jnp.bfloat16
    deep = half + 2
    starts = [0] + [lines * (b + 1) + 2 for b in range(chunks)]
    cuts = starts[:-1] + [half + 1]
    offset = 1 - part

    loads = [
        pltpu.make_async_copy(source, target, load_sem.at[i])
        for i, (source, target) in enumerate(
            (
                (
                    video_hbm.at[:, pl.ds((half - 1) * part, half + 1)],
                    video.at[pl.ds(2 + frames * part, frames), pl.ds(offset, half + 1)],
                ),
                (wt_hbm, wt), (wd_hbm, wd), (ws_hbm, ws),
                (wq_hbm, wq), (wk_hbm, wk), (wv_hbm, wv), (wo_hbm, wo),
            )
        )
    ]
    for load in loads:
        load.start()

    barrier = pltpu.get_barrier_semaphore()

    def greet(k, _):
        peer = lax.rem(me + k, owners)
        pl.semaphore_signal(barrier, inc=1, device_id={"tm": peer}, device_id_type=MESH)
        return 0

    lax.fori_loop(1, owners, greet, 0)

    def greet_side(k, _):
        peer = lax.rem(col + k, cols)
        pl.semaphore_signal(barrier, inc=1, device_id={"cols": peer}, device_id_type=MESH)
        return 0

    lax.fori_loop(1, cols, greet_side, 0)

    upper, lower = part == 0, part == 1
    has_next, has_before = group < groups - 1, group > 0
    starts_clip = group == 0
    slots = video.shape[0]
    for part_of, line in ((upper, 0), (lower, deep - 1)):
        @pl.when(part_of)
        def _():
            video[:, line] = jnp.zeros((slots, strip, channels), bf16)

    @pl.when(starts_clip)
    def _():
        video[0:2] = jnp.zeros((2, deep, strip, channels), bf16)
        lifted[0] = jnp.zeros((deep, strip, channels), bf16)

    @pl.when(jnp.logical_not(has_next))
    def _():
        video[slots - 2 :] = jnp.zeros((2, deep, strip, channels), bf16)

    pl.semaphore_wait(barrier, owners + cols - 2)

    def remote(source, target, sent, landed, peer):
        return pltpu.make_async_remote_copy(
            src_ref=source, dst_ref=target, send_sem=sent, recv_sem=landed,
            device_id={"tm": peer}, device_id_type=MESH,
        )

    def trade(i, b):
        first, count = ((frames - 2) * part, 2) if i == 0 else (2 * (1 - part), frames - 2)
        size = cuts[b + 1] - cuts[b]
        return remote(
            video_hbm.at[pl.ds(first, count), pl.ds((half - 1) * (1 - part) + cuts[b], size)],
            video.at[pl.ds(2 + frames * part + first, count), pl.ds(part + cuts[b], size)],
            trade_send.at[i, b], trade_recv.at[i, b], me + 1 - 2 * part,
        )

    def upward(b):
        size = pl.ds(offset + cuts[b], cuts[b + 1] - cuts[b])
        peer = lax.rem(me + 2, owners)
        return remote(video.at[2 * frames + 1, size], video.at[1, size], up_send.at[b], up_recv.at[b], peer)

    def downward(b):
        size = pl.ds(offset + cuts[b], cuts[b + 1] - cuts[b])
        peer = lax.rem(me + owners - 2, owners)
        return remote(
            video.at[pl.ds(2, 2), size], video.at[pl.ds(slots - 2, 2), size],
            down_send.at[b], down_recv.at[b], peer,
        )

    def send_up(b):
        @pl.when(has_next)
        def _():
            upward(b).start()

    def send_down(b):
        @pl.when(has_before)
        def _():
            downward(b).start()

    def pass_on(b):
        trade(0, b).wait_recv()

        @pl.when(upper)
        def _():
            send_up(b)

        @pl.when(lower)
        def _():
            send_down(b)

    def stacked(ref, which, b):
        size = (starts[b + 1] - starts[b]) * strip
        return jnp.concatenate(
            [ref[f, starts[b] : starts[b + 1]].reshape(size, channels) for f in which], 0
        )

    def lift(which, b):
        count = starts[b + 1] - starts[b]
        size = count * strip
        own = [f + 2 for f in which]
        summed = jnp.dot(stacked(video, own, b), wt[0], preferred_element_type=f32)
        for k in (1, 2):
            summed = summed + jnp.dot(
                stacked(video, [f - k for f in own], b), wt[k], preferred_element_type=f32
            )
        summed = summed + bt[...]
        result = (stacked(video, own, b).astype(f32) + jax.nn.silu(summed)).astype(bf16)
        for i, f in enumerate(which):
            lifted[f + 1, starts[b] : starts[b + 1]] = result[i * size : (i + 1) * size].reshape(
                count, strip, channels
            )

    def sideways(low, b, side):
        peer = lax.rem(col + 1, cols) if side == 0 else lax.rem(col + cols - 1, cols)
        which = pl.ds(low, ours + 1 - low)
        return pltpu.make_async_remote_copy(
            src_ref=edges.at[b, side, which], dst_ref=halo.at[b, side, which],
            send_sem=edge_send.at[b, side], recv_sem=edge_recv.at[b, side],
            device_id={"cols": peer}, device_id_type=MESH,
        )

    sends_side = (col < cols - 1, col > 0)
    takes_side = (col > 0, col < cols - 1)

    def reduce_band(low, b):
        first, last = starts[b], starts[b + 1]
        count, many = last - first, ours + 1 - low
        which = range(low, ours + 1)
        summed = jnp.zeros((many * count * strip, channels), f32) + bd[...]
        for k in range(3):
            summed = summed + jnp.dot(
                stacked(lifted, [2 * j + 2 - k for j in which], b), wd[k], preferred_element_type=f32
            )
        middle[low:, first:last] = summed.astype(bf16).reshape(many, count, strip, channels)
        if b == 0:
            @pl.when(upper)
            def _():
                middle[low:, 0] = jnp.zeros((many, strip, channels), bf16)
        if b == chunks - 1:
            @pl.when(lower)
            def _():
                middle[low:, deep - 1] = jnp.zeros((many, strip, channels), bf16)
        wide = middle[low:, first:last].astype(f32)
        rest = jnp.zeros((many, padded - count, channels), f32)
        for side, place in ((0, strip - 1), (1, 0)):
            column = wide[:, :, place]
            column = jnp.concatenate([column, rest], 1) if padded > count else column
            edges[b, side, low:] = column.astype(bf16)
        for side in range(2):
            @pl.when(sends_side[side])
            def _():
                sideways(low, b, side).start()

    def shift_band(low, b):
        first, last = starts[b], starts[b + 1]
        count, many = last - first, ours + 1 - low
        size = many * count * strip
        for side in range(2):
            @pl.when(takes_side[side])
            def _():
                sideways(low, b, side).wait_recv()

            @pl.when(jnp.logical_not(takes_side[side]))
            def _():
                halo[b, side, low:] = jnp.zeros((many, padded, channels), bf16)

        wide = middle[low:, first:last].reshape(size, channels).astype(f32)
        place = lax.rem(lax.broadcasted_iota(jnp.int32, (size, channels), 0), strip)

        def spread(side):
            column = halo[b, side, low:].astype(f32)[:, :count]
            column = jnp.broadcast_to(column[:, :, None, :], (many, count, strip, channels))
            return column.reshape(size, channels)

        before = jnp.where(place == 0, spread(0), pltpu.roll(wide, 1, 0))
        after = jnp.where(place == strip - 1, spread(1), pltpu.roll(wide, size - 1, 0))
        left_of[low:, first:last] = before.astype(bf16).reshape(many, count, strip, channels)
        right_of[low:, first:last] = after.astype(bf16).reshape(many, count, strip, channels)

    def convolve_band(low, c):
        first, many = c * lines, ours + 1 - low

        def window(ref, a):
            return ref[low:, first + a : first + a + lines].reshape(many * lines * strip, channels)

        summed = jnp.zeros((many * lines * strip, channels), f32) + bs[...]
        for k, shifted in ((1, middle), (0, left_of), (2, right_of)):
            for a in range(3):
                summed = summed + jnp.dot(
                    window(shifted, a), ws[3 * a + k], preferred_element_type=f32
                )
        result = (window(middle, 1).astype(f32) + jax.nn.silu(summed)).astype(bf16)
        result = result.reshape(many, groups, pixels, channels)
        for j in range(many):
            spatial[c, :, low + j] = result[j]

    def by_group(which, act):
        @pl.when(which == 0)
        def _():
            act(0, ours + 1)

        @pl.when((which > 0) & (which < groups - 1))
        def _():
            act(1, ours)

        @pl.when(which == groups - 1)
        def _():
            act(1, ours - 1)

    def outward(low, count, c, peer, slot, source):
        first = ours * source + 1 if low else 0
        return remote(
            spatial.at[c, peer, pl.ds(low, count)], held.at[c, pl.ds(first, count)],
            send_sem.at[c, slot], recv_sem.at[c, source], 2 * peer + part,
        )

    def homeward(c, peer, slot, source, side, line):
        return remote(
            done.at[c, peer], y_ref.at[:, side, c, line], back_sem.at[c, slot], home_sem.at[c, source], peer
        )

    def scatter(c):
        def act(low, count):
            def send(k, _):
                outward(low, count, c, lax.rem(group + k, groups), k, group).start()
                return 0

            lax.fori_loop(1, groups, send, 0)

        by_group(group, act)

    def attend(c):
        def keep(low, count):
            first = ours * group + 1 if low else 0
            held[c, pl.ds(first, count)] = spatial[c, group, low : low + count]

        by_group(group, keep)

        def arrive(k, _):
            source = lax.rem(group + groups - k, groups)

            def act(low, count):
                outward(low, count, c, lax.rem(group + k, groups), k, source).wait_recv()

            by_group(source, act)
            return 0

        lax.fori_loop(1, groups, arrive, 0)
        place = lax.broadcasted_iota(jnp.int32, (rows, rows), 0)
        other = lax.broadcasted_iota(jnp.int32, (rows, rows), 1)
        allowed = (lax.rem(place, pixels) == lax.rem(other, pixels)) & (other <= place)
        wide = held[c].reshape(rows, channels).astype(f32)
        scale = lax.rsqrt(jnp.mean(wide * wide, axis=-1, keepdims=True) + epsilon)
        normed = (wide * scale * gain[...]).astype(bf16)
        query = jnp.dot(normed, wq[...], preferred_element_type=f32).astype(bf16)
        key = jnp.dot(normed, wk[...], preferred_element_type=f32).astype(bf16)
        value = jnp.dot(normed, wv[...], preferred_element_type=f32).astype(bf16)
        scores = lax.dot_general(
            query, key, (((1,), (1,)), ((), ())), preferred_element_type=f32
        ) * channels ** (-0.5)
        scores = jnp.where(allowed, scores, -1e30)
        largest = jnp.max(scores, axis=-1, keepdims=True)
        probs = jnp.exp(scores - largest)
        probs = (probs / jnp.sum(probs, axis=-1, keepdims=True)).astype(bf16)
        context = jnp.dot(probs, value, preferred_element_type=f32).astype(bf16)
        mixed = jnp.dot(context, wo[...], preferred_element_type=f32)
        result = (wide + mixed).astype(bf16)
        done[c] = result.reshape(owners, halves, pixels, channels)

        def back(k, _):
            homeward(c, lax.rem(me + k, owners), k, me, part, group).start()
            return 0

        lax.fori_loop(1, owners, back, 0)
        y_ref[:, part, c, group] = done[c, me]

    for b in range(chunks):
        for i in range(2):
            trade(i, b).start()
    loads[0].wait()
    for b in range(chunks):
        @pl.when(lower)
        def _():
            send_up(b)

        @pl.when(upper)
        def _():
            send_down(b)
    for load in loads[1:]:
        load.wait()

    last = 2 * frames
    pass_on(0)
    for b in range(chunks):
        trade(1, b).wait_recv()

        def band(low):
            lift(range(2 * low, last), b)
            if low:
                upward(b).wait_recv()

            @pl.when(has_next)
            def _():
                downward(b).wait_recv()

            lift(([1] if low else []) + [last, last + 1], b)
            reduce_band(low, b)
            if b + 1 < chunks:
                pass_on(b + 1)
            shift_band(low, b)
            convolve_band(low, b)

        @pl.when(starts_clip)
        def _():
            band(0)

        @pl.when(has_before)
        def _():
            band(1)

        scatter(b)
    for c in range(chunks):
        attend(c)

    for b in range(chunks):
        for i in range(2):
            trade(i, b).wait_send()

        @pl.when(has_next)
        def _():
            upward(b).wait_send()

        @pl.when(has_before)
        def _():
            downward(b).wait_send()

        for low, chosen in ((0, starts_clip), (1, has_before)):
            for side in range(2):
                @pl.when(sends_side[side] & chosen)
                def _():
                    sideways(low, b, side).wait_send()

    for c in range(chunks):
        def left(low, count):
            def sent(k, _):
                outward(low, count, c, lax.rem(group + k, groups), k, group).wait_send()
                return 0

            lax.fori_loop(1, groups, sent, 0)

        by_group(group, left)

        def finish(k, _):
            peer, source = lax.rem(me + k, owners), lax.rem(me + owners - k, owners)
            homeward(c, peer, k, me, part, group).wait_send()
            homeward(c, peer, k, source, lax.rem(source, 2), lax.div(source, 2)).wait_recv()
            return 0

        lax.fori_loop(1, owners, finish, 0)


def per_device(
    video, w_time, b_time, w_down, b_down, w_space, b_space, gain, w_query, w_key, w_value, w_out
):
    frames, height, strip, channels = video.shape
    halves, owners = frames // 2, lax.axis_size("tm")
    groups, half = owners // 2, height // 2
    owned = half * strip // groups
    pixels = min(16, owned)
    chunks = owned // pixels
    deep, slots = half + 2, 2 * halves + 1
    padded = -(-(half // chunks + 2) // 8) * 8
    vmem = pl.BlockSpec(memory_space=pltpu.VMEM)
    hbm = pl.BlockSpec(memory_space=pltpu.HBM)
    bf16 = jnp.bfloat16
    square = (channels, channels)
    shifted = pltpu.VMEM((slots, deep, strip, channels), bf16)
    flat = lambda v: v.reshape(1, channels)
    sems = pltpu.SemaphoreType.DMA
    result = pl.pallas_call(
        block_kernel,
        out_shape=jax.ShapeDtypeStruct((halves, 2, chunks, groups, pixels, channels), bf16),
        in_specs=[hbm, hbm, vmem, hbm, vmem, hbm, vmem, vmem, hbm, hbm, hbm, hbm],
        out_specs=vmem,
        scratch_shapes=[
            pltpu.VMEM((3,) + square, bf16),
            pltpu.VMEM((3,) + square, bf16),
            pltpu.VMEM((9,) + square, bf16),
            pltpu.VMEM(square, bf16),
            pltpu.VMEM(square, bf16),
            pltpu.VMEM(square, bf16),
            pltpu.VMEM(square, bf16),
            pltpu.VMEM((2 * frames + 4, deep, strip, channels), bf16),
            pltpu.VMEM((2 * frames + 3, deep, strip, channels), bf16),
            shifted,
            shifted,
            shifted,
            pltpu.VMEM((chunks, 2, slots, padded, channels), bf16),
            pltpu.VMEM((chunks, 2, slots, padded, channels), bf16),
            pltpu.VMEM((chunks, groups, slots, pixels, channels), bf16),
            pltpu.VMEM((chunks, owners * halves, pixels, channels), bf16),
            pltpu.VMEM((chunks, owners, halves, pixels, channels), bf16),
            sems((8,)),
            sems((2, chunks)),
            sems((2, chunks)),
            sems((chunks,)),
            sems((chunks,)),
            sems((chunks,)),
            sems((chunks,)),
            sems((chunks, 2)),
            sems((chunks, 2)),
            sems((chunks, groups)),
            sems((chunks, groups)),
            sems((chunks, owners)),
            sems((chunks, owners)),
        ],
        compiler_params=pltpu.CompilerParams(
            collective_id=0, has_side_effects=True, vmem_limit_bytes=57 * 1024 * 1024
        ),
    )(
        video, w_time, flat(b_time), w_down, flat(b_down),
        w_space, flat(b_space), flat(gain), w_query, w_key, w_value, w_out,
    )
    return result.reshape(halves, height, strip, channels)


def solution(mesh):
    return jax.shard_map(
        per_device,
        mesh=mesh,
        in_specs=(P(("clips", "tm"), None, "cols", None),) + (P(),) * 11,
        out_specs=P(("clips", "tm"), None, "cols", None),
        check_vma=False,
    )
```

time: 89.4 us -> 79.2 us (0.89)
  Pallas kernels: 86.9 us -> 76.8 us
    pallas_call x1, Pallas kernels: 86.9 us -> 76.8 us  [per_device(): pl.pallas_call(block_kernel, out_shape=jax.ShapeDtypeStruct((halves, 2, c...]
where the time goes in v2:
time: 79.2 us; the launch traced here: 79.1 us
  Pallas kernels  76.8 us (97%)
  local copies, waits for them, and re-layouts  2.26 us (3%)
    pallas_call x1, Pallas kernels, per_device(): pl.pallas_call(block_kernel, out_shape=jax.ShapeDtypeStruct((halves, 2, c...  76.8 us
    unnamed x1, local copies, waits for them, and re-layouts  2.26 us

profile of v2, /device:TPU:27, one launch (start us, length us, event | category | flops | bytes accessed | tf_op | source)
XLA Modules:
  0.0 79.1 jit_solution(9151488807255370611)
XLA Ops:
  0.0 76.8 %shard_map.118 = bf16[2,2,4,4,16,512]{5,4,3,2,1,0:T(8,128)(2,1)} custom-call(bf16[4,32,16,512]{3,2,1,0:T(8,128)(2,1)} %video_hbm.1, bf16[3,512,512]{2,1,0:T(8,128)(2,1)} %wt_hbm.1, f32[1,512]{1,0:T(1,128)} %bitcast.6, bf16[3,512,512]{2,1,0:T(8,128)(2,1)} %wd_hbm.1, f32[1,512]{1,0:T(1,128)} %bitcast.7, bf16[9,512,512]{2,1,0:T(8,128)(2,1)} %ws_hbm.1, ...), custom_call_target="tpu_custom_call" | custom-call | tf_op jit(solution)/shard_map/pallas_call | solution.py:425
  76.8 2.3 %copy.14 = bf16[2,32,16,512]{3,2,1,0:T(8,128)(2,1)} copy(bf16[2,32,16,512]{3,2,1,0:T(8,128)(2,1)} %bitcast.5) | data formatting | bytes 2097152

commit v3 on v2

--- a/solution.py
+++ b/solution.py
@@ -14,7 +14,7 @@
     wt, wd, ws, wq, wk, wv, wo, video, lifted, left_of, middle, right_of,
     edges, halo, spatial, held, done,
     load_sem, trade_send, trade_recv, up_send, up_recv, down_send, down_recv, edge_send, edge_recv,
-    send_sem, recv_sem, back_sem, home_sem,
+    send_sem, recv_sem, tail_send, tail_recv, head_send, head_recv, back_sem, home_sem,
 ):
     frames, height, strip, channels = video_hbm.shape
     halves, _, chunks, groups, pixels, _ = y_ref.shape
@@ -24,6 +24,7 @@
     half = height // 2
     lines = half // chunks
     padded = edges.shape[3]
+    joint = 2 if chunks % 2 == 0 else 1
     me, col, cols = lax.axis_index("tm"), lax.axis_index("cols"), lax.axis_size("cols")
     group, part = lax.div(me, 2), lax.rem(me, 2)
     f32, bf16 = jnp.float32, jnp.bfloat16
@@ -133,130 +134,128 @@
         def _():
             send_down(b)
 
-    def stacked(ref, which, b):
-        size = (starts[b + 1] - starts[b]) * strip
-        return jnp.concatenate(
-            [ref[f, starts[b] : starts[b + 1]].reshape(size, channels) for f in which], 0
-        )
-
-    def lift(which, b):
-        count = starts[b + 1] - starts[b]
+    def stacked(ref, which, first, last):
+        size = (last - first) * strip
+        return jnp.concatenate([ref[f, first:last].reshape(size, channels) for f in which], 0)
+
+    def lift(which, first, last):
+        count = last - first
         size = count * strip
         own = [f + 2 for f in which]
-        summed = jnp.dot(stacked(video, own, b), wt[0], preferred_element_type=f32)
+        summed = jnp.dot(stacked(video, own, first, last), wt[0], preferred_element_type=f32)
         for k in (1, 2):
             summed = summed + jnp.dot(
-                stacked(video, [f - k for f in own], b), wt[k], preferred_element_type=f32
+                stacked(video, [f - k for f in own], first, last), wt[k], preferred_element_type=f32
             )
         summed = summed + bt[...]
-        result = (stacked(video, own, b).astype(f32) + jax.nn.silu(summed)).astype(bf16)
+        result = (stacked(video, own, first, last).astype(f32) + jax.nn.silu(summed)).astype(bf16)
         for i, f in enumerate(which):
-            lifted[f + 1, starts[b] : starts[b + 1]] = result[i * size : (i + 1) * size].reshape(
-                count, strip, channels
-            )
-
-    def sideways(low, b, side):
+            lifted[f + 1, first:last] = result[i * size : (i + 1) * size].reshape(count, strip, channels)
+
+    def sideways(step, many, side):
         peer = lax.rem(col + 1, cols) if side == 0 else lax.rem(col + cols - 1, cols)
-        which = pl.ds(low, ours + 1 - low)
+        which = pl.ds(0, many)
         return pltpu.make_async_remote_copy(
-            src_ref=edges.at[b, side, which], dst_ref=halo.at[b, side, which],
-            send_sem=edge_send.at[b, side], recv_sem=edge_recv.at[b, side],
+            src_ref=edges.at[step, side, which], dst_ref=halo.at[step, side, which],
+            send_sem=edge_send.at[step, side], recv_sem=edge_recv.at[step, side],
             device_id={"cols": peer}, device_id_type=MESH,
         )
 
     sends_side = (col < cols - 1, col > 0)
     takes_side = (col > 0, col < cols - 1)
 
-    def reduce_band(low, b):
-        first, last = starts[b], starts[b + 1]
-        count, many = last - first, ours + 1 - low
-        which = range(low, ours + 1)
-        summed = jnp.zeros((many * count * strip, channels), f32) + bd[...]
+    def reduce_rows(step, which, first, last):
+        count, many = last - first, len(which)
+        size = count * strip
+        summed = jnp.zeros((many * size, channels), f32) + bd[...]
         for k in range(3):
             summed = summed + jnp.dot(
-                stacked(lifted, [2 * j + 2 - k for j in which], b), wd[k], preferred_element_type=f32
+                stacked(lifted, [2 * j + 2 - k for j in which], first, last), wd[k],
+                preferred_element_type=f32,
             )
-        middle[low:, first:last] = summed.astype(bf16).reshape(many, count, strip, channels)
-        if b == 0:
-            @pl.when(upper)
-            def _():
-                middle[low:, 0] = jnp.zeros((many, strip, channels), bf16)
-        if b == chunks - 1:
-            @pl.when(lower)
-            def _():
-                middle[low:, deep - 1] = jnp.zeros((many, strip, channels), bf16)
-        wide = middle[low:, first:last].astype(f32)
+        reduced = summed.astype(bf16)
+        for i, j in enumerate(which):
+            middle[j, first:last] = reduced[i * size : (i + 1) * size].reshape(count, strip, channels)
+            for chosen, line in ((upper, 0), (lower, deep - 1)):
+                if first <= line < last:
+                    @pl.when(chosen)
+                    def _():
+                        middle[j, line] = jnp.zeros((strip, channels), bf16)
+        wide = stacked(middle, which, first, last).astype(f32).reshape(many, count, strip, channels)
         rest = jnp.zeros((many, padded - count, channels), f32)
         for side, place in ((0, strip - 1), (1, 0)):
             column = wide[:, :, place]
             column = jnp.concatenate([column, rest], 1) if padded > count else column
-            edges[b, side, low:] = column.astype(bf16)
+            edges[step, side, :many] = column.astype(bf16)
         for side in range(2):
             @pl.when(sends_side[side])
             def _():
-                sideways(low, b, side).start()
-
-    def shift_band(low, b):
-        first, last = starts[b], starts[b + 1]
-        count, many = last - first, ours + 1 - low
-        size = many * count * strip
+                sideways(step, many, side).start()
+
+    def shift_rows(step, which, first, last):
+        count, many = last - first, len(which)
+        part_size = count * strip
+        size = many * part_size
         for side in range(2):
             @pl.when(takes_side[side])
             def _():
-                sideways(low, b, side).wait_recv()
+                sideways(step, many, side).wait_recv()
 
             @pl.when(jnp.logical_not(takes_side[side]))
             def _():
-                halo[b, side, low:] = jnp.zeros((many, padded, channels), bf16)
-
-        wide = middle[low:, first:last].reshape(size, channels).astype(f32)
+                halo[step, side, :many] = jnp.zeros((many, padded, channels), bf16)
+
+        wide = stacked(middle, which, first, last).astype(f32)
         place = lax.rem(lax.broadcasted_iota(jnp.int32, (size, channels), 0), strip)
 
         def spread(side):
-            column = halo[b, side, low:].astype(f32)[:, :count]
+            column = halo[step, side, :many].astype(f32)[:, :count]
             column = jnp.broadcast_to(column[:, :, None, :], (many, count, strip, channels))
             return column.reshape(size, channels)
 
-        before = jnp.where(place == 0, spread(0), pltpu.roll(wide, 1, 0))
-        after = jnp.where(place == strip - 1, spread(1), pltpu.roll(wide, size - 1, 0))
-        left_of[low:, first:last] = before.astype(bf16).reshape(many, count, strip, channels)
-        right_of[low:, first:last] = after.astype(bf16).reshape(many, count, strip, channels)
-
-    def convolve_band(low, c):
-        first, many = c * lines, ours + 1 - low
+        before = jnp.where(place == 0, spread(0), pltpu.roll(wide, 1, 0)).astype(bf16)
+        after = jnp.where(place == strip - 1, spread(1), pltpu.roll(wide, size - 1, 0)).astype(bf16)
+        for i, j in enumerate(which):
+            own = slice(i * part_size, (i + 1) * part_size)
+            left_of[j, first:last] = before[own].reshape(count, strip, channels)
+            right_of[j, first:last] = after[own].reshape(count, strip, channels)
+
+    def convolve_chunks(which, first, count):
+        top, deep_rows = first * lines, count * lines
+        many = len(which)
 
         def window(ref, a):
-            return ref[low:, first + a : first + a + lines].reshape(many * lines * strip, channels)
-
-        summed = jnp.zeros((many * lines * strip, channels), f32) + bs[...]
+            return stacked(ref, which, top + a, top + a + deep_rows)
+
+        summed = jnp.zeros((many * deep_rows * strip, channels), f32) + bs[...]
         for k, shifted in ((1, middle), (0, left_of), (2, right_of)):
             for a in range(3):
                 summed = summed + jnp.dot(
                     window(shifted, a), ws[3 * a + k], preferred_element_type=f32
                 )
         result = (window(middle, 1).astype(f32) + jax.nn.silu(summed)).astype(bf16)
-        result = result.reshape(many, groups, pixels, channels)
-        for j in range(many):
-            spatial[c, :, low + j] = result[j]
-
-    def by_group(which, act):
-        @pl.when(which == 0)
-        def _():
-            act(0, ours + 1)
-
-        @pl.when((which > 0) & (which < groups - 1))
-        def _():
-            act(1, ours)
-
-        @pl.when(which == groups - 1)
-        def _():
-            act(1, ours - 1)
-
-    def outward(low, count, c, peer, slot, source):
-        first = ours * source + 1 if low else 0
+        result = result.reshape(many, count, groups, pixels, channels)
+        for i, j in enumerate(which):
+            for c in range(count):
+                spatial[first + c, :, j] = result[i, c]
+
+    def outward(c, peer, slot, source):
+        count = ours - 1
         return remote(
-            spatial.at[c, peer, pl.ds(low, count)], held.at[c, pl.ds(first, count)],
+            spatial.at[c, peer, pl.ds(1, count)], held.at[c, pl.ds(ours * source + 1, count)],
             send_sem.at[c, slot], recv_sem.at[c, source], 2 * peer + part,
+        )
+
+    def tailward(c, peer, slot, source):
+        frame = lax.rem(ours * (source + 1), total)
+        return remote(
+            spatial.at[c, peer, ours], held.at[c, frame],
+            tail_send.at[c, slot], tail_recv.at[c, source], 2 * peer + part,
+        )
+
+    def headward(c, peer, slot):
+        return remote(
+            spatial.at[c, peer, 0], held.at[c, 0], head_send.at[c, slot], head_recv.at[c], 2 * peer + part
         )
 
     def homeward(c, peer, slot, source, side, line):
@@ -264,33 +263,49 @@
             done.at[c, peer], y_ref.at[:, side, c, line], back_sem.at[c, slot], home_sem.at[c, source], peer
         )
 
+    def others(act):
+        def step(k, _):
+            act(k, lax.rem(group + k, groups), lax.rem(group + groups - k, groups))
+            return 0
+
+        lax.fori_loop(1, groups, step, 0)
+
     def scatter(c):
-        def act(low, count):
-            def send(k, _):
-                outward(low, count, c, lax.rem(group + k, groups), k, group).start()
-                return 0
-
-            lax.fori_loop(1, groups, send, 0)
-
-        by_group(group, act)
+        others(lambda k, peer, source: outward(c, peer, k, group).start())
+
+    def scatter_late(c):
+        @pl.when(has_next)
+        def _():
+            others(lambda k, peer, source: tailward(c, peer, k, group).start())
+
+        @pl.when(starts_clip)
+        def _():
+            others(lambda k, peer, source: headward(c, peer, k).start())
 
     def attend(c):
-        def keep(low, count):
-            first = ours * group + 1 if low else 0
-            held[c, pl.ds(first, count)] = spatial[c, group, low : low + count]
-
-        by_group(group, keep)
-
-        def arrive(k, _):
-            source = lax.rem(group + groups - k, groups)
-
-            def act(low, count):
-                outward(low, count, c, lax.rem(group + k, groups), k, source).wait_recv()
-
-            by_group(source, act)
-            return 0
-
-        lax.fori_loop(1, groups, arrive, 0)
+        held[c, pl.ds(ours * group + 1, ours - 1)] = spatial[c, group, 1:ours]
+
+        @pl.when(has_next)
+        def _():
+            held[c, ours * group + ours] = spatial[c, group, ours]
+
+        @pl.when(starts_clip)
+        def _():
+            held[c, 0] = spatial[c, group, 0]
+
+        def arrive(k, peer, source):
+            outward(c, peer, k, source).wait_recv()
+
+            @pl.when(source < groups - 1)
+            def _():
+                tailward(c, peer, k, source).wait_recv()
+
+        others(arrive)
+
+        @pl.when(has_before)
+        def _():
+            headward(c, 0, 0).wait_recv()
+
         place = lax.broadcasted_iota(jnp.int32, (rows, rows), 0)
         other = lax.broadcasted_iota(jnp.int32, (rows, rows), 1)
         allowed = (lax.rem(place, pixels) == lax.rem(other, pixels)) & (other <= place)
@@ -334,36 +349,51 @@
     for load in loads[1:]:
         load.wait()
 
-    last = 2 * frames
+    final = 2 * frames
+    main, ends = tuple(range(1, ours)), (0, ours)
+    steps = chunks + chunks // joint
+
+    def late(step, which, lifts, first):
+        span = starts[first], starts[first + joint]
+        lift(lifts, *span)
+        reduce_rows(step, which, *span)
+        shift_rows(step, which, *span)
+        convolve_chunks(which, first, joint)
+
     pass_on(0)
     for b in range(chunks):
         trade(1, b).wait_recv()
 
-        def band(low):
-            lift(range(2 * low, last), b)
-            if low:
-                upward(b).wait_recv()
+        @pl.when(has_before)
+        def _():
+            upward(b).wait_recv()
+
+        lift(range(1, final), starts[b], starts[b + 1])
+        reduce_rows(b, main, starts[b], starts[b + 1])
+        shift_rows(b, main, starts[b], starts[b + 1])
+        convolve_chunks(main, b, 1)
+        if b + 1 < chunks:
+            pass_on(b + 1)
+        scatter(b)
+        if (b + 1) % joint == 0:
+            first = b + 1 - joint
+            step = chunks + first // joint
 
             @pl.when(has_next)
             def _():
-                downward(b).wait_recv()
-
-            lift(([1] if low else []) + [last, last + 1], b)
-            reduce_band(low, b)
-            if b + 1 < chunks:
-                pass_on(b + 1)
-            shift_band(low, b)
-            convolve_band(low, b)
-
-        @pl.when(starts_clip)
-        def _():
-            band(0)
-
-        @pl.when(has_before)
-        def _():
-            band(1)
-
-        scatter(b)
+                for d in range(first, first + joint):
+                    downward(d).wait_recv()
+
+            @pl.when(starts_clip)
+            def _():
+                late(step, ends, (0, final, final + 1), first)
+
+            @pl.when(has_before & has_next)
+            def _():
+                late(step, ends[1:], (final, final + 1), first)
+
+            for c in range(first, first + joint):
+                scatter_late(c)
     for c in range(chunks):
         attend(c)
 
@@ -379,21 +409,26 @@
         def _():
             downward(b).wait_send()
 
-        for low, chosen in ((0, starts_clip), (1, has_before)):
+    for step in range(steps):
+        kinds = ((len(main), col >= 0),)
+        if step >= chunks:
+            kinds = ((2, starts_clip), (1, has_before & has_next))
+        for many, chosen in kinds:
             for side in range(2):
                 @pl.when(sends_side[side] & chosen)
                 def _():
-                    sideways(low, b, side).wait_send()
+                    sideways(step, many, side).wait_send()
 
     for c in range(chunks):
-        def left(low, count):
-            def sent(k, _):
-                outward(low, count, c, lax.rem(group + k, groups), k, group).wait_send()
-                return 0
-
-            lax.fori_loop(1, groups, sent, 0)
-
-        by_group(group, left)
+        others(lambda k, peer, source: outward(c, peer, k, group).wait_send())
+
+        @pl.when(has_next)
+        def _():
+            others(lambda k, peer, source: tailward(c, peer, k, group).wait_send())
+
+        @pl.when(starts_clip)
+        def _():
+            others(lambda k, peer, source: headward(c, peer, k).wait_send())
 
         def finish(k, _):
             peer, source = lax.rem(me + k, owners), lax.rem(me + owners - k, owners)
@@ -414,7 +449,9 @@
     pixels = min(16, owned)
     chunks = owned // pixels
     deep, slots = half + 2, 2 * halves + 1
-    padded = -(-(half // chunks + 2) // 8) * 8
+    joint = 2 if chunks % 2 == 0 else 1
+    padded = -(-(joint * half // chunks + 2) // 8) * 8
+    steps = chunks + chunks // joint
     vmem = pl.BlockSpec(memory_space=pltpu.VMEM)
     hbm = pl.BlockSpec(memory_space=pltpu.HBM)
     bf16 = jnp.bfloat16
@@ -440,8 +477,8 @@
             shifted,
             shifted,
             shifted,
-            pltpu.VMEM((chunks, 2, slots, padded, channels), bf16),
-            pltpu.VMEM((chunks, 2, slots, padded, channels), bf16),
+            pltpu.VMEM((steps, 2, slots, padded, channels), bf16),
+            pltpu.VMEM((steps, 2, slots, padded, channels), bf16),
             pltpu.VMEM((chunks, groups, slots, pixels, channels), bf16),
             pltpu.VMEM((chunks, owners * halves, pixels, channels), bf16),
             pltpu.VMEM((chunks, owners, halves, pixels, channels), bf16),
@@ -452,10 +489,14 @@
             sems((chunks,)),
             sems((chunks,)),
             sems((chunks,)),
-            sems((chunks, 2)),
-            sems((chunks, 2)),
+            sems((steps, 2)),
+            sems((steps, 2)),
             sems((chunks, groups)),
             sems((chunks, groups)),
+            sems((chunks, groups)),
+            sems((chunks, groups)),
+            sems((chunks, groups)),
+            sems((chunks,)),
             sems((chunks, owners)),
             sems((chunks, owners)),
         ],

time: 79.2 us -> 81.3 us (1.027)
  the two profiles are of different devices: /device:TPU:27 before, /device:TPU:0 now
where the time goes in v3:
time: 81.3 us; the launch traced here: 81.1 us
  Pallas kernels  78.8 us (97%)
  local copies, waits for them, and re-layouts  2.26 us (3%)
    pallas_call x1, Pallas kernels, per_device(): pl.pallas_call(block_kernel, out_shape=jax.ShapeDtypeStruct((halves, 2, c...  78.8 us
    unnamed x1, local copies, waits for them, and re-layouts  2.26 us

profile of v3, /device:TPU:0, one launch (start us, length us, event | category | flops | bytes accessed | tf_op | source)
XLA Modules:
  0.0 81.1 jit_solution(8634709070168851597)
XLA Ops:
  0.0 78.8 %shard_map.118 = bf16[2,2,4,4,16,512]{5,4,3,2,1,0:T(8,128)(2,1)} custom-call(bf16[4,32,16,512]{3,2,1,0:T(8,128)(2,1)} %video_hbm.1, bf16[3,512,512]{2,1,0:T(8,128)(2,1)} %wt_hbm.1, f32[1,512]{1,0:T(1,128)} %bitcast.6, bf16[3,512,512]{2,1,0:T(8,128)(2,1)} %wd_hbm.1, f32[1,512]{1,0:T(1,128)} %bitcast.7, bf16[9,512,512]{2,1,0:T(8,128)(2,1)} %ws_hbm.1, ...), custom_call_target="tpu_custom_call" | custom-call | tf_op jit(solution)/shard_map/pallas_call | solution.py:462
  78.8 2.3 %copy.14 = bf16[2,32,16,512]{3,2,1,0:T(8,128)(2,1)} copy(bf16[2,32,16,512]{3,2,1,0:T(8,128)(2,1)} %bitcast.5) | data formatting | bytes 2097152

commit v4 on v3

--- a/solution.py
+++ b/solution.py
@@ -15,9 +15,10 @@
     edges, halo, spatial, held, done,
     load_sem, trade_send, trade_recv, up_send, up_recv, down_send, down_recv, edge_send, edge_recv,
     send_sem, recv_sem, tail_send, tail_recv, head_send, head_recv, back_sem, home_sem,
+    from_below, from_above, from_partner,
 ):
     frames, height, strip, channels = video_hbm.shape
-    halves, _, chunks, groups, pixels, _ = y_ref.shape
+    _, chunks, groups, halves, pixels, _ = y_ref.shape
     owners, ours = 2 * groups, 2 * halves
     total = groups * ours
     rows = total * pixels
@@ -32,6 +33,7 @@
     starts = [0] + [lines * (b + 1) + 2 for b in range(chunks)]
     cuts = starts[:-1] + [half + 1]
     offset = 1 - part
+    lead = min(1, chunks)
 
     loads = [
         pltpu.make_async_copy(source, target, load_sem.at[i])
@@ -51,12 +53,23 @@
 
     barrier = pltpu.get_barrier_semaphore()
 
-    def greet(k, _):
-        peer = lax.rem(me + k, owners)
-        pl.semaphore_signal(barrier, inc=1, device_id={"tm": peer}, device_id_type=MESH)
-        return 0
-
-    lax.fori_loop(1, owners, greet, 0)
+    upper, lower = part == 0, part == 1
+    has_next, has_before = group < groups - 1, group > 0
+
+    def tell(semaphore, peer):
+        pl.semaphore_signal(semaphore, inc=1, device_id={"tm": peer}, device_id_type=MESH)
+
+    partner = me + 1 - 2 * part
+    above, below = lax.rem(me + 2, owners), lax.rem(me + owners - 2, owners)
+    tell(barrier, partner)
+
+    @pl.when(has_next)
+    def _():
+        tell(barrier, above)
+
+    @pl.when(has_before)
+    def _():
+        tell(barrier, below)
 
     def greet_side(k, _):
         peer = lax.rem(col + k, cols)
@@ -65,8 +78,6 @@
 
     lax.fori_loop(1, cols, greet_side, 0)
 
-    upper, lower = part == 0, part == 1
-    has_next, has_before = group < groups - 1, group > 0
     starts_clip = group == 0
     slots = video.shape[0]
     for part_of, line in ((upper, 0), (lower, deep - 1)):
@@ -83,7 +94,7 @@
     def _():
         video[slots - 2 :] = jnp.zeros((2, deep, strip, channels), bf16)
 
-    pl.semaphore_wait(barrier, owners + cols - 2)
+    pl.semaphore_wait(barrier, cols + jnp.where(has_next, 1, 0) + jnp.where(has_before, 1, 0))
 
     def remote(source, target, sent, landed, peer):
         return pltpu.make_async_remote_copy(
@@ -92,7 +103,7 @@
         )
 
     def trade(i, b):
-        first, count = ((frames - 2) * part, 2) if i == 0 else (2 * (1 - part), frames - 2)
+        first, count = (frames - 1, 1) if i == 0 else (0, frames - 1)
         size = cuts[b + 1] - cuts[b]
         return remote(
             video_hbm.at[pl.ds(first, count), pl.ds((half - 1) * (1 - part) + cuts[b], size)],
@@ -123,13 +134,15 @@
         def _():
             downward(b).start()
 
-    def pass_on(b):
-        trade(0, b).wait_recv()
-
-        @pl.when(upper)
-        def _():
-            send_up(b)
-
+    def pass_up(b):
+        if b < chunks:
+            trade(0, b).wait_recv()
+
+            @pl.when(upper)
+            def _():
+                send_up(b)
+
+    def pass_down(b):
         @pl.when(lower)
         def _():
             send_down(b)
@@ -260,8 +273,11 @@
 
     def homeward(c, peer, slot, source, side, line):
         return remote(
-            done.at[c, peer], y_ref.at[:, side, c, line], back_sem.at[c, slot], home_sem.at[c, source], peer
-        )
+            done.at[c, peer], y_ref.at[side, c, line], back_sem.at[c, slot], home_sem.at[c, source], peer
+        )
+
+    def stay(c):
+        return pltpu.make_async_copy(done.at[c, me], y_ref.at[part, c, group], home_sem.at[c, me])
 
     def others(act):
         def step(k, _):
@@ -332,11 +348,13 @@
             return 0
 
         lax.fori_loop(1, owners, back, 0)
-        y_ref[:, part, c, group] = done[c, me]
-
-    for b in range(chunks):
-        for i in range(2):
-            trade(i, b).start()
+        stay(c).start()
+
+    for b in range(chunks + lead):
+        if b < chunks:
+            trade(0, b).start()
+        if b >= lead:
+            trade(1, b - lead).start()
     loads[0].wait()
     for b in range(chunks):
         @pl.when(lower)
@@ -348,6 +366,20 @@
             send_down(b)
     for load in loads[1:]:
         load.wait()
+
+    for first, then, semaphore, peer in (
+        (has_before, has_next, from_below, above), (has_next, has_before, from_above, below)
+    ):
+        @pl.when(first)
+        def _():
+            pl.semaphore_wait(semaphore, 1)
+
+        @pl.when(then)
+        def _():
+            tell(semaphore, peer)
+
+    tell(from_partner, partner)
+    pl.semaphore_wait(from_partner, 1)
 
     final = 2 * frames
     main, ends = tuple(range(1, ours)), (0, ours)
@@ -360,9 +392,12 @@
         shift_rows(step, which, *span)
         convolve_chunks(which, first, joint)
 
-    pass_on(0)
+    for b in range(lead):
+        pass_up(b)
     for b in range(chunks):
+        pass_up(b + lead)
         trade(1, b).wait_recv()
+        pass_down(b)
 
         @pl.when(has_before)
         def _():
@@ -372,29 +407,29 @@
         reduce_rows(b, main, starts[b], starts[b + 1])
         shift_rows(b, main, starts[b], starts[b + 1])
         convolve_chunks(main, b, 1)
-        if b + 1 < chunks:
-            pass_on(b + 1)
         scatter(b)
-        if (b + 1) % joint == 0:
-            first = b + 1 - joint
-            step = chunks + first // joint
-
-            @pl.when(has_next)
-            def _():
-                for d in range(first, first + joint):
-                    downward(d).wait_recv()
-
-            @pl.when(starts_clip)
-            def _():
-                late(step, ends, (0, final, final + 1), first)
-
-            @pl.when(has_before & has_next)
-            def _():
-                late(step, ends[1:], (final, final + 1), first)
-
-            for c in range(first, first + joint):
-                scatter_late(c)
-    for c in range(chunks):
+    for first in range(0, chunks, joint):
+        step = chunks + first // joint
+
+        @pl.when(has_next)
+        def _():
+            for d in range(first, first + joint):
+                downward(d).wait_recv()
+
+        @pl.when(starts_clip)
+        def _():
+            late(step, ends, (0, final, final + 1), first)
+
+        @pl.when(has_before & has_next)
+        def _():
+            late(step, ends[1:], (final, final + 1), first)
+
+        for c in range(first, first + joint):
+            scatter_late(c)
+        if first:
+            for c in range(first - joint, first):
+                attend(c)
+    for c in range(chunks - joint, chunks):
         attend(c)
 
     for b in range(chunks):
@@ -437,6 +472,7 @@
             return 0
 
         lax.fori_loop(1, owners, finish, 0)
+        stay(c).wait()
 
 
 def per_device(
@@ -461,9 +497,9 @@
     sems = pltpu.SemaphoreType.DMA
     result = pl.pallas_call(
         block_kernel,
-        out_shape=jax.ShapeDtypeStruct((halves, 2, chunks, groups, pixels, channels), bf16),
+        out_shape=jax.ShapeDtypeStruct((2, chunks, groups, halves, pixels, channels), bf16),
         in_specs=[hbm, hbm, vmem, hbm, vmem, hbm, vmem, vmem, hbm, hbm, hbm, hbm],
-        out_specs=vmem,
+        out_specs=hbm,
         scratch_shapes=[
             pltpu.VMEM((3,) + square, bf16),
             pltpu.VMEM((3,) + square, bf16),
@@ -499,6 +535,9 @@
             sems((chunks,)),
             sems((chunks, owners)),
             sems((chunks, owners)),
+            pltpu.SemaphoreType.REGULAR,
+            pltpu.SemaphoreType.REGULAR,
+            pltpu.SemaphoreType.REGULAR,
         ],
         compiler_params=pltpu.CompilerParams(
             collective_id=0, has_side_effects=True, vmem_limit_bytes=57 * 1024 * 1024
@@ -507,7 +546,7 @@
         video, w_time, flat(b_time), w_down, flat(b_down),
         w_space, flat(b_space), flat(gain), w_query, w_key, w_value, w_out,
     )
-    return result.reshape(halves, height, strip, channels)
+    return result.transpose(3, 0, 1, 2, 4, 5).reshape(halves, height, strip, channels)
 
 
 def solution(mesh):

time: 81.3 us -> 77 us (0.947)
  the two profiles are of different devices: /device:TPU:0 before, /device:TPU:27 now
where the time goes in v4:
time: 77 us; the launch traced here: 76.8 us
  Pallas kernels  74.5 us (97%)
  local copies, waits for them, and re-layouts  2.28 us (3%)
    pallas_call x1, Pallas kernels, per_device(): pl.pallas_call(block_kernel, out_shape=jax.ShapeDtypeStruct((2, chunks, g...  74.5 us
    reshape x1, local copies, waits for them, and re-layouts, per_device(): result.transpose(3, 0, 1, 2, 4, 5).reshape(halves, height, strip, channels)  2.28 us

profile of v4, /device:TPU:27, one launch (start us, length us, event | category | flops | bytes accessed | tf_op | source)
XLA Modules:
  0.0 76.8 jit_solution(11635402028345556037)
XLA Ops:
  0.0 74.5 %shard_map.118 = bf16[2,4,4,2,16,512]{5,4,3,2,1,0:T(8,128)(2,1)} custom-call(bf16[4,32,16,512]{3,2,1,0:T(8,128)(2,1)} %video_hbm.1, bf16[3,512,512]{2,1,0:T(8,128)(2,1)} %wt_hbm.1, f32[1,512]{1,0:T(1,128)} %bitcast.8, bf16[3,512,512]{2,1,0:T(8,128)(2,1)} %wd_hbm.1, f32[1,512]{1,0:T(1,128)} %bitcast.9, bf16[9,512,512]{2,1,0:T(8,128)(2,1)} %ws_hbm.1, ...), custom_call_target="tpu_custom_call" | custom-call | tf_op jit(solution)/shard_map/pallas_call | solution.py:498
  74.5 2.3 %copy.13 = bf16[2,32,16,512]{3,2,1,0:T(8,128)(2,1)} copy(bf16[2,32,16,512]{3,2,0,1:T(8,128)(2,1)} %bitcast.7) | data formatting | bytes 2097152 | tf_op jit(solution)/shard_map/reshape | solution.py:549

commit v5 on v4

--- a/solution.py
+++ b/solution.py
@@ -350,11 +350,9 @@
         lax.fori_loop(1, owners, back, 0)
         stay(c).start()
 
-    for b in range(chunks + lead):
-        if b < chunks:
-            trade(0, b).start()
-        if b >= lead:
-            trade(1, b - lead).start()
+    for b in range(chunks):
+        for i in range(2):
+            trade(i, b).start()
     loads[0].wait()
     for b in range(chunks):
         @pl.when(lower)
@@ -392,10 +390,11 @@
         shift_rows(step, which, *span)
         convolve_chunks(which, first, joint)
 
-    for b in range(lead):
-        pass_up(b)
+    pass_up(0)
+    ready = [frames * part + f for f in range(2, frames)]
+    waiting = [1, frames, frames + 1] + [frames * (1 - part) + f for f in range(2, frames)]
+    lift(ready, 0, deep)
     for b in range(chunks):
-        pass_up(b + lead)
         trade(1, b).wait_recv()
         pass_down(b)
 
@@ -403,8 +402,9 @@
         def _():
             upward(b).wait_recv()
 
-        lift(range(1, final), starts[b], starts[b + 1])
+        lift(waiting, starts[b], starts[b + 1])
         reduce_rows(b, main, starts[b], starts[b + 1])
+        pass_up(b + 1)
         shift_rows(b, main, starts[b], starts[b + 1])
         convolve_chunks(main, b, 1)
         scatter(b)

time: 77 us -> 76.2 us (0.990); the launches traced: 76.8 us -> 75 us
  Pallas kernels: 74.5 us -> 72.7 us
    pallas_call x1, Pallas kernels: 74.5 us -> 72.7 us  [per_device(): pl.pallas_call(block_kernel, out_shape=jax.ShapeDtypeStruct((2, chunks, g...]
where the time goes in v5:
time: 76.2 us; the launch traced here: 75 us
  Pallas kernels  72.7 us (95%)
  local copies, waits for them, and re-layouts  2.28 us (3%)
    pallas_call x1, Pallas kernels, per_device(): pl.pallas_call(block_kernel, out_shape=jax.ShapeDtypeStruct((2, chunks, g...  72.7 us
    reshape x1, local copies, waits for them, and re-layouts, per_device(): result.transpose(3, 0, 1, 2, 4, 5).reshape(halves, height, strip, channels)  2.28 us

profile of v5, /device:TPU:27, one launch (start us, length us, event | category | flops | bytes accessed | tf_op | source)
XLA Modules:
  0.0 75.0 jit_solution(8069486644602963470)
XLA Ops:
  0.0 72.7 %shard_map.118 = bf16[2,4,4,2,16,512]{5,4,3,2,1,0:T(8,128)(2,1)} custom-call(bf16[4,32,16,512]{3,2,1,0:T(8,128)(2,1)} %video_hbm.1, bf16[3,512,512]{2,1,0:T(8,128)(2,1)} %wt_hbm.1, f32[1,512]{1,0:T(1,128)} %bitcast.8, bf16[3,512,512]{2,1,0:T(8,128)(2,1)} %wd_hbm.1, f32[1,512]{1,0:T(1,128)} %bitcast.9, bf16[9,512,512]{2,1,0:T(8,128)(2,1)} %ws_hbm.1, ...), custom_call_target="tpu_custom_call" | custom-call | tf_op jit(solution)/shard_map/pallas_call | solution.py:498
  72.7 2.3 %copy.13 = bf16[2,32,16,512]{3,2,1,0:T(8,128)(2,1)} copy(bf16[2,32,16,512]{3,2,0,1:T(8,128)(2,1)} %bitcast.7) | data formatting | bytes 2097152 | tf_op jit(solution)/shard_map/reshape | solution.py:549

commit v6 on v5

--- a/solution.py
+++ b/solution.py
@@ -281,7 +281,7 @@
 
     def others(act):
         def step(k, _):
-            act(k, lax.rem(group + k, groups), lax.rem(group + groups - k, groups))
+            act(k, lax.rem(group + groups - k, groups), lax.rem(group + k, groups))
             return 0
 
         lax.fori_loop(1, groups, step, 0)

time: 76.2 us -> 75.1 us (0.986)
  Pallas kernels: 72.7 us -> 71.5 us
    pallas_call x1, Pallas kernels: 72.7 us -> 71.5 us  [per_device(): pl.pallas_call(block_kernel, out_shape=jax.ShapeDtypeStruct((2, chunks, g...]
where the time goes in v6:
time: 75.1 us; the launch traced here: 73.8 us
  Pallas kernels  71.5 us (95%)
  local copies, waits for them, and re-layouts  2.28 us (3%)
    pallas_call x1, Pallas kernels, per_device(): pl.pallas_call(block_kernel, out_shape=jax.ShapeDtypeStruct((2, chunks, g...  71.5 us
    reshape x1, local copies, waits for them, and re-layouts, per_device(): result.transpose(3, 0, 1, 2, 4, 5).reshape(halves, height, strip, channels)  2.28 us

profile of v6, /device:TPU:27, one launch (start us, length us, event | category | flops | bytes accessed | tf_op | source)
XLA Modules:
  0.0 73.8 jit_solution(17869045903779226482)
XLA Ops:
  0.0 71.5 %shard_map.118 = bf16[2,4,4,2,16,512]{5,4,3,2,1,0:T(8,128)(2,1)} custom-call(bf16[4,32,16,512]{3,2,1,0:T(8,128)(2,1)} %video_hbm.1, bf16[3,512,512]{2,1,0:T(8,128)(2,1)} %wt_hbm.1, f32[1,512]{1,0:T(1,128)} %bitcast.8, bf16[3,512,512]{2,1,0:T(8,128)(2,1)} %wd_hbm.1, f32[1,512]{1,0:T(1,128)} %bitcast.9, bf16[9,512,512]{2,1,0:T(8,128)(2,1)} %ws_hbm.1, ...), custom_call_target="tpu_custom_call" | custom-call | tf_op jit(solution)/shard_map/pallas_call | solution.py:498
  71.5 2.3 %copy.13 = bf16[2,32,16,512]{3,2,1,0:T(8,128)(2,1)} copy(bf16[2,32,16,512]{3,2,0,1:T(8,128)(2,1)} %bitcast.7) | data formatting | bytes 2097152 | tf_op jit(solution)/shard_map/reshape | solution.py:549
